TPU v7x, 32 devices: a whole 2x2x4 slice. The times are simulated.
32 devices in a mesh: dp: 8 (over z, y), tensor: 4 (over x, core).
Axes of the slice: x: 2, y: 2, z: 4, core: 2. Of those that a mesh axis runs over, the one named last changes fastest.
Arguments:
- tokens: bfloat16 [16384, 768], P(('dp', 'tensor'))
- first_values: bfloat16 [16384, 384], P(('dp', 'tensor')), may hold values from -6 to 6
- pieces: int32 [16384], P('dp'), may hold values from 0 to 64, as said below
- lengths: int32 [8], P('dp'), may hold values from 256 to 2048, as said below
- w_query: bfloat16 [768, 768], P('dp', 'tensor'), may hold values from -0.21875 to 0.21875
- w_key: bfloat16 [768, 768], P('dp', 'tensor'), may hold values from -0.21875 to 0.21875
- w_value: bfloat16 [768, 384], P('dp'), may hold values from -0.21875 to 0.21875
- w_out: bfloat16 [768, 768], P('tensor', 'dp'), may hold values from -2.5 to 2.5
- w_up: bfloat16 [768, 3072], P('dp', 'tensor'), may hold values from -0.21875 to 0.21875
- w_down: bfloat16 [3072, 768], P('tensor', 'dp'), may hold values from -0.15625 to 0.15625
- gain_attn: float32 [768], replicated, may hold values from 0.1 to 1.9
- gain_mlp: float32 [768], replicated, may hold values from 0.1 to 1.9
- cotangent: bfloat16 [16384, 768], P(('dp', 'tensor')), may hold values from -6 to 6
Outputs:
- output: bfloat16 [16384, 768], P(('dp', 'tensor'))
- d_tokens: float32 [16384, 768], P(('dp', 'tensor'))
- d_first_values: float32 [16384, 384], P(('dp', 'tensor'))
- d_w_query: float32 [768, 768], P('dp', 'tensor')
- d_w_key: float32 [768, 768], P('dp', 'tensor')
- d_w_value: float32 [768, 384], P('dp')
- d_w_out: float32 [768, 768], P('tensor', 'dp')
- d_w_up: float32 [768, 3072], P('dp', 'tensor')
- d_w_down: float32 [3072, 768], P('tensor', 'dp')
- d_gain_attn: float32 [768], replicated
- d_gain_mlp: float32 [768], replicated
- rms: float32 [3], replicated
Inputs may be any that keep to these rules, and one draw needn't show every extreme that they name: `pieces`: each aligned block of 256 tokens carries one number: 0 for text, or a positive number that no other block carries, for a picture piece. `lengths`: 2048 is reached in every draw.
All inputs are finite; a program needn't handle non-finite values.
Results may differ from a plain program's by a relative error of at most 0.018.
Values may be sent and summed in bfloat16 or wider, within the bound.
No kernel may reach another device: no remote copies, remote signals or barrier semaphores. Data moves between devices by JAX's collectives and lax.ppermute only.
A program may use at most 256 MiB of HBM per device.

v0:
```python
import math
import jax
import jax.numpy as jnp
from jax import lax
from jax.sharding import PartitionSpec as P

HD = 64
EPS = 1e-05
NEG = -1e30


def matmul(first_op, second_op):
    return jnp.dot(first_op, second_op, preferred_element_type=jnp.float32)


def matmul_tn(first_op, second_op):
    return lax.dot_general(
        first_op, second_op, (((0,), (0,)), ((), ())), preferred_element_type=jnp.float32
    )


def matmul_nt(first_op, second_op):
    return lax.dot_general(
        first_op, second_op, (((1,), (1,)), ((), ())), preferred_element_type=jnp.float32
    )


def norm_forward(resid, norm_gain):
    centred = resid - jnp.mean(resid, axis=-1, keepdims=True)
    inv_std = lax.rsqrt(jnp.mean(centred * centred, axis=-1, keepdims=True) + EPS)
    normed = centred * inv_std
    return (normed * norm_gain, normed, inv_std)


def norm_backward(upstream, norm_gain, normed, inv_std):
    scaled = upstream * norm_gain
    inner = (
        scaled
        - jnp.mean(scaled, axis=-1, keepdims=True)
        - normed * jnp.mean(scaled * normed, axis=-1, keepdims=True)
    )
    return (inner * inv_std, jnp.sum(upstream * normed, axis=0))


def visible_mask(pieces, valid_len, q_start, q_count, k_count):
    q_pos = q_start + lax.iota(jnp.int32, q_count)
    k_pos = lax.iota(jnp.int32, k_count)
    q_piece = pieces[q_start : q_start + q_count]
    k_piece = pieces[:k_count]
    same_piece = (q_piece[:, None] == k_piece[None, :]) & (q_piece[:, None] > 0)
    causal = k_pos[None, :] <= q_pos[:, None]
    return (k_pos[None, :] < valid_len) & (causal | same_piece)


def attend_forward(queries, key_rows, value_rows, pieces, valid_len):
    seq_len, head_cols = queries.shape
    local_heads = head_cols // HD
    scale_factor = 1.0 / math.sqrt(HD)
    block_rows = min(512, seq_len // 2)
    q_split = queries.reshape(seq_len, local_heads, HD)
    k_split = key_rows.reshape(seq_len, local_heads, HD)
    v_split = value_rows.reshape(seq_len, local_heads, HD)
    outputs = []
    log_sums = []
    for block_idx in range(seq_len // block_rows):
        q_start = block_idx * block_rows
        q_stop = q_start + block_rows
        raw_scores = (
            jnp.einsum(
                "qhd,khd->hqk",
                q_split[q_start:q_stop],
                k_split[:q_stop],
                preferred_element_type=jnp.float32,
            )
            * scale_factor
        )
        scores = jnp.where(
            visible_mask(pieces, valid_len, q_start, block_rows, q_stop)[None], raw_scores, NEG
        )
        row_max = jnp.max(scores, axis=-1, keepdims=True)
        exp_scores = jnp.exp(scores - row_max)
        row_total = jnp.sum(exp_scores, axis=-1, keepdims=True)
        attn_probs = (exp_scores / row_total).astype(jnp.bfloat16)
        head_out = jnp.einsum(
            "hqk,khd->qhd", attn_probs, v_split[:q_stop], preferred_element_type=jnp.float32
        )
        outputs.append(head_out.reshape(block_rows, head_cols).astype(jnp.bfloat16))
        log_sums.append(row_max + jnp.log(row_total))
    return (jnp.concatenate(outputs, axis=0), log_sums)


def attend_backward(queries, key_rows, value_rows, grad_heads, log_sums, pieces, valid_len):
    seq_len, head_cols = queries.shape
    local_heads = head_cols // HD
    scale_factor = 1.0 / math.sqrt(HD)
    block_rows = min(512, seq_len // 2)
    q_split = queries.reshape(seq_len, local_heads, HD)
    k_split = key_rows.reshape(seq_len, local_heads, HD)
    v_split = value_rows.reshape(seq_len, local_heads, HD)
    g_split = grad_heads.reshape(seq_len, local_heads, HD)
    grad_keys = jnp.zeros((seq_len, local_heads, HD), jnp.float32)
    grad_vals = jnp.zeros((seq_len, local_heads, HD), jnp.float32)
    grad_q_blocks = []
    for block_idx in range(seq_len // block_rows):
        q_start = block_idx * block_rows
        q_stop = q_start + block_rows
        q_block = q_split[q_start:q_stop]
        g_block = g_split[q_start:q_stop]
        raw_scores = (
            jnp.einsum(
                "qhd,khd->hqk", q_block, k_split[:q_stop], preferred_element_type=jnp.float32
            )
            * scale_factor
        )
        scores = jnp.where(
            visible_mask(pieces, valid_len, q_start, block_rows, q_stop)[None], raw_scores, NEG
        )
        attn_probs = jnp.exp(scores - log_sums[block_idx])
        low_probs = attn_probs.astype(jnp.bfloat16)
        grad_vals = grad_vals.at[:q_stop].add(
            jnp.einsum("hqk,qhd->khd", low_probs, g_block, preferred_element_type=jnp.float32)
        )
        grad_probs = jnp.einsum(
            "qhd,khd->hqk", g_block, v_split[:q_stop], preferred_element_type=jnp.float32
        )
        inner_sum = jnp.sum(attn_probs * grad_probs, axis=-1, keepdims=True)
        grad_scores = (attn_probs * (grad_probs - inner_sum)).astype(jnp.bfloat16)
        grad_q_blocks.append(
            jnp.einsum(
                "hqk,khd->qhd", grad_scores, k_split[:q_stop], preferred_element_type=jnp.float32
            )
            * scale_factor
        )
        grad_keys = grad_keys.at[:q_stop].add(
            jnp.einsum("hqk,qhd->khd", grad_scores, q_block, preferred_element_type=jnp.float32)
            * scale_factor
        )
    grad_q = jnp.concatenate(grad_q_blocks, axis=0).reshape(seq_len, head_cols)
    return (grad_q, grad_keys.reshape(seq_len, head_cols), grad_vals.reshape(seq_len, head_cols))


def gelu_tanh(pre_act):
    return jax.nn.gelu(pre_act, approximate=True)


def body(
    tokens,
    first_values,
    pieces,
    lengths,
    w_query,
    w_key,
    w_value,
    w_out,
    w_up,
    w_down,
    gain_attn,
    gain_mlp,
    cotangent,
):
    tensor_size = lax.axis_size("tensor")
    tensor_rank = lax.axis_index("tensor")
    fresh_ranks = tensor_size // 2
    local_rows, model_dim = tokens.shape
    seq_len = local_rows * tensor_size
    head_cols = w_query.shape[1]
    value_width = w_value.shape[1]
    valid_len = lengths[0]
    positions = tensor_rank * local_rows + lax.iota(jnp.int32, local_rows)
    valid = (positions < valid_len).astype(jnp.float32)[:, None]
    query_w, key_w, value_w, out_w, up_w, down_w = (
        lax.all_gather(w_query, "dp", axis=0, tiled=True),
        lax.all_gather(w_key, "dp", axis=0, tiled=True),
        lax.all_gather(w_value, "dp", axis=0, tiled=True),
        lax.all_gather(w_out, "dp", axis=1, tiled=True),
        lax.all_gather(w_up, "dp", axis=0, tiled=True),
        lax.all_gather(w_down, "dp", axis=1, tiled=True),
    )
    tokens_wide = tokens.astype(jnp.float32)
    norm_one, normed_one, inv_one = norm_forward(tokens_wide, gain_attn)
    attn_input = norm_one.astype(jnp.bfloat16)
    input_rows, first_rows = (
        lax.all_gather(attn_input, "tensor", axis=0, tiled=True),
        lax.all_gather(first_values, "tensor", axis=0, tiled=True),
    )
    queries = matmul(input_rows, query_w).astype(jnp.bfloat16)
    key_rows = matmul(input_rows, key_w).astype(jnp.bfloat16)

    def fresh_values(rows_in):
        value_cols = lax.dynamic_slice_in_dim(value_w, tensor_rank * head_cols, head_cols, 1)
        return matmul(rows_in, value_cols).astype(jnp.bfloat16)

    def reused_values(rows_in):
        return lax.dynamic_slice_in_dim(
            first_rows, (tensor_rank - fresh_ranks) * head_cols, head_cols, 1
        )

    value_rows = lax.cond(tensor_rank < fresh_ranks, fresh_values, reused_values, input_rows)
    heads_out, log_sums = attend_forward(queries, key_rows, value_rows, pieces, valid_len)
    attn_out = lax.psum_scatter(
        matmul(heads_out, out_w).astype(jnp.bfloat16), "tensor", scatter_dimension=0, tiled=True
    ).astype(jnp.float32)
    resid_mid = tokens_wide + attn_out
    norm_two, normed_two, inv_two = norm_forward(resid_mid, gain_mlp)
    mlp_input = norm_two.astype(jnp.bfloat16)
    mlp_rows = lax.all_gather(mlp_input, "tensor", axis=0, tiled=True)
    up_pre = matmul(mlp_rows, up_w)
    hidden_act, gelu_pull = jax.vjp(gelu_tanh, up_pre)
    hidden = hidden_act.astype(jnp.bfloat16)
    mlp_out = lax.psum_scatter(
        matmul(hidden, down_w).astype(jnp.bfloat16), "tensor", scatter_dimension=0, tiled=True
    ).astype(jnp.float32)
    final = resid_mid + mlp_out
    squares = jnp.stack(
        [
            jnp.sum(valid * final * final),
            jnp.sum(valid * attn_out * attn_out),
            jnp.sum(valid * mlp_out * mlp_out),
            jnp.sum(valid),
        ]
    )
    query_w, key_w, value_w, out_w, up_w, down_w = (
        lax.all_gather(w_query, "dp", axis=0, tiled=True),
        lax.all_gather(w_key, "dp", axis=0, tiled=True),
        lax.all_gather(w_value, "dp", axis=0, tiled=True),
        lax.all_gather(w_out, "dp", axis=1, tiled=True),
        lax.all_gather(w_up, "dp", axis=0, tiled=True),
        lax.all_gather(w_down, "dp", axis=1, tiled=True),
    )
    out_grad = cotangent.astype(jnp.float32)
    cot_rows = lax.all_gather(cotangent, "tensor", axis=0, tiled=True)
    grad_down_w = matmul_tn(hidden, cot_rows)
    grad_hidden = matmul_nt(cot_rows, down_w)
    grad_up_pre = gelu_pull(grad_hidden)[0].astype(jnp.bfloat16)
    grad_up_w = matmul_tn(mlp_rows, grad_up_pre)
    grad_mlp_input = lax.psum_scatter(
        matmul_nt(grad_up_pre, up_w).astype(jnp.bfloat16), "tensor", scatter_dimension=0, tiled=True
    ).astype(jnp.float32)
    grad_two, gain_two_grad = norm_backward(grad_mlp_input, gain_mlp, normed_two, inv_two)
    resid_grad = out_grad + grad_two
    resid_rows = lax.all_gather(resid_grad.astype(jnp.bfloat16), "tensor", axis=0, tiled=True)
    grad_out_w = matmul_tn(heads_out, resid_rows)
    grad_heads = matmul_nt(resid_rows, out_w).astype(jnp.bfloat16)
    grad_q, grad_k, grad_v = attend_backward(
        queries, key_rows, value_rows, grad_heads, log_sums, pieces, valid_len
    )
    grad_q_low = grad_q.astype(jnp.bfloat16)
    grad_k_low = grad_k.astype(jnp.bfloat16)
    grad_query_w = matmul_tn(input_rows, grad_q_low)
    grad_key_w = matmul_tn(input_rows, grad_k_low)
    input_part = matmul_nt(grad_q_low, query_w) + matmul_nt(grad_k_low, key_w)

    def fresh_back(grad_vals):
        grad_low = grad_vals.astype(jnp.bfloat16)
        value_cols = lax.dynamic_slice_in_dim(value_w, tensor_rank * head_cols, head_cols, 1)
        grad_cols = matmul_tn(input_rows, grad_low)
        grad_value_full = lax.dynamic_update_slice_in_dim(
            jnp.zeros((model_dim, value_width), jnp.float32), grad_cols, tensor_rank * head_cols, 1
        )
        return (
            grad_value_full,
            matmul_nt(grad_low, value_cols),
            jnp.zeros((seq_len, value_width), jnp.float32),
        )

    def reused_back(grad_vals):
        first_part = lax.dynamic_update_slice_in_dim(
            jnp.zeros((seq_len, value_width), jnp.float32),
            grad_vals,
            (tensor_rank - fresh_ranks) * head_cols,
            1,
        )
        return (
            jnp.zeros((model_dim, value_width), jnp.float32),
            jnp.zeros((seq_len, model_dim), jnp.float32),
            first_part,
        )

    grad_value_w, value_input, first_part = lax.cond(
        tensor_rank < fresh_ranks, fresh_back, reused_back, grad_v
    )
    grad_attn_input, first_grad = (
        lax.psum_scatter(
            (input_part + value_input).astype(jnp.bfloat16),
            "tensor",
            scatter_dimension=0,
            tiled=True,
        ).astype(jnp.float32),
        lax.psum_scatter(
            first_part.astype(jnp.bfloat16), "tensor", scatter_dimension=0, tiled=True
        ).astype(jnp.float32),
    )
    grad_one, gain_one_grad = norm_backward(grad_attn_input, gain_attn, normed_one, inv_one)
    token_grad = resid_grad + grad_one
    grad_query_w, grad_key_w, grad_out_w, grad_up_w, grad_down_w = (
        lax.psum_scatter(grad_query_w, "dp", scatter_dimension=0, tiled=True),
        lax.psum_scatter(grad_key_w, "dp", scatter_dimension=0, tiled=True),
        lax.psum_scatter(grad_out_w, "dp", scatter_dimension=1, tiled=True),
        lax.psum_scatter(grad_up_w, "dp", scatter_dimension=0, tiled=True),
        lax.psum_scatter(grad_down_w, "dp", scatter_dimension=1, tiled=True),
    )
    value_total, gain_one_total, gain_two_total, square_total = lax.psum(
        (grad_value_w, gain_one_grad, gain_two_grad, squares), ("dp", "tensor")
    )
    share_rows = value_total.shape[0] // lax.axis_size("dp")
    value_share = lax.dynamic_slice_in_dim(
        value_total, lax.axis_index("dp") * share_rows, share_rows, 0
    )
    rms = jnp.sqrt(square_total[:3] / (square_total[3] * model_dim))
    return (
        final.astype(jnp.bfloat16),
        token_grad,
        first_grad,
        grad_query_w,
        grad_key_w,
        value_share,
        grad_out_w,
        grad_up_w,
        grad_down_w,
        gain_one_total,
        gain_two_total,
        rms,
    )


def solution(mesh):
    in_specs = (
        P(("dp", "tensor"), None),
        P(("dp", "tensor"), None),
        P("dp"),
        P("dp"),
        P("dp", "tensor"),
        P("dp", "tensor"),
        P("dp", None),
        P("tensor", "dp"),
        P("dp", "tensor"),
        P("tensor", "dp"),
        P(),
        P(),
        P(("dp", "tensor"), None),
    )
    out_specs = (
        P(("dp", "tensor"), None),
        P(("dp", "tensor"), None),
        P(("dp", "tensor"), None),
        P("dp", "tensor"),
        P("dp", "tensor"),
        P("dp", None),
        P("tensor", "dp"),
        P("dp", "tensor"),
        P("tensor", "dp"),
        P(),
        P(),
        P(),
    )
    return jax.shard_map(body, mesh=mesh, in_specs=in_specs, out_specs=out_specs, check_vma=False)
```

profile of v0, /device:TPU:0, one launch (start us, length us, event | category | flops | bytes accessed | tf_op | source)
XLA Modules:
  0.0 1069.0 jit_solution(11694905929463329441)
XLA Ops:
  16.4 35.0 %all_gather.44 = bf16[192,768]{0,1:T(8,128)(2,1)} all-gather(bf16[192,96]{0,1:T(8,128)(2,1)S(1)} %copy.36), channel_id=1, replica_groups=mesh['dp'=8,'tensor'=4] {'dp'}, dimensions={1}, use_global_device_ids=true | all-gather | bytes 331776 | tf_op jit(solution)/shard_map/all_gather | solution.py:175
  51.4 31.3 %all_gather.42 = bf16[768,192]{1,0:T(8,128)(2,1)S(1)} all-gather(bf16[96,192]{1,0:T(8,128)(2,1)S(1)} %copy-done.70), channel_id=1, replica_groups=mesh['dp'=8,'tensor'=4] {'dp'}, dimensions={0}, use_global_device_ids=true | all-gather | bytes 331776 | tf_op jit(solution)/shard_map/all_gather | solution.py:172
  82.6 31.0 %all_gather.43 = bf16[768,192]{1,0:T(8,128)(2,1)S(1)} all-gather(bf16[96,192]{1,0:T(8,128)(2,1)S(1)} %copy-done.71), channel_id=1, replica_groups=mesh['dp'=8,'tensor'=4] {'dp'}, dimensions={0}, use_global_device_ids=true | all-gather | bytes 331776 | tf_op jit(solution)/shard_map/all_gather | solution.py:173
  116.2 33.7 %all_gather.40 = bf16[768,384]{1,0:T(8,128)(2,1)} all-gather(bf16[96,384]{1,0:T(8,128)(2,1)S(1)} %copy-done.63), channel_id=1, replica_groups=mesh['dp'=8,'tensor'=4] {'dp'}, dimensions={0}, use_global_device_ids=true | all-gather | bytes 663552 | tf_op jit(solution)/shard_map/all_gather | solution.py:174
  196.3 36.2 %reduce-scatter.13.cloned.1.call-done = bf16[512,768]{1,0:T(8,128)(2,1)} async-done(((bf16[2048,768]{1,0:T(8,128)(2,1)}), bf16[512,768]{1,0:T(8,128)(2,1)}) %reduce-scatter.13.cloned.1.call-update) | async-done | bytes 786448 | tf_op jit(solution)/shard_map/reduce_scatter | solution.py:200
  238.8 28.4 %all-gather.18.cloned.1.call-done = bf16[2048,768]{1,0:T(8,128)(2,1)} async-done(((bf16[512,768]{1,0:T(8,128)(2,1)}), bf16[2048,768]{1,0:T(8,128)(2,1)}) %all-gather.18.cloned.1.call-update) | async-done | bytes 3145744 | tf_op jit(solution)/shard_map/all_gather | solution.py:231
  267.2 7.4 fusion.135
  274.6 36.4 %all-gather.14.cloned.1.call-done = bf16[768,768]{1,0:T(8,128)(2,1)} async-done(((bf16[96,768]{1,0:T(8,128)(2,1)}), bf16[768,768]{1,0:T(8,128)(2,1)}) %all-gather.14.cloned.1.call-update) | async-done | bytes 1179664 | tf_op jit(solution)/shard_map/all_gather | solution.py:176
  311.1 29.1 %all-gather.12.cloned.1.call-done = bf16[2048,768]{1,0:T(8,128)(2,1)} async-done(((bf16[512,768]{1,0:T(8,128)(2,1)}), bf16[2048,768]{1,0:T(8,128)(2,1)}) %all-gather.12.cloned.1.call-update) | async-done | bytes 3145744 | tf_op jit(solution)/shard_map/all_gather | solution.py:206
  340.2 10.0 fusion.17
  357.2 8.3 convolution_convert_fusion.2
  365.8 28.3 %reduce-scatter.17.cloned.1.call-done = bf16[512,768]{1,0:T(8,128)(2,1)} async-done(((bf16[2048,768]{1,0:T(8,128)(2,1)}), bf16[512,768]{1,0:T(8,128)(2,1)}) %reduce-scatter.17.cloned.1.call-update) | async-done | bytes 786448 | tf_op jit(solution)/shard_map/reduce_scatter | solution.py:236
  394.1 40.4 %reduce-scatter.15.cloned.1.call-done = bf16[512,768]{1,0:T(8,128)(2,1)} async-done(((bf16[2048,768]{1,0:T(8,128)(2,1)}), bf16[512,768]{1,0:T(8,128)(2,1)}) %reduce-scatter.15.cloned.1.call-update) | async-done | bytes 786448 | tf_op jit(solution)/shard_map/reduce_scatter | solution.py:210
  442.3 28.3 %all-gather.20.cloned.1.call-done = bf16[2048,768]{1,0:T(8,128)(2,1)} async-done(((bf16[512,768]{1,0:T(8,128)(2,1)}), bf16[2048,768]{1,0:T(8,128)(2,1)}) %all-gather.20.cloned.1.call-update) | async-done | bytes 3145744 | tf_op jit(solution)/shard_map/all_gather | solution.py:241
  478.1 8.9 multiply_reduce_fusion.1
  493.5 17.0 %conditional.3 = (f32[768,384]{0,1:T(8,128)}, bf16[2048,384]{1,0:T(8,128)(2,1)S(1)}, f32[2048,768]{1,0:T(8,128)}) conditional(s32[]{:T(128)} %convert_element_type.169, (s32[]{:T(128)}, bf16[2048,192]{0,1:T(8,128)(2,1)S(1)}) %tuple.159, (bf16[2048,192]{0,1:T(8,128)(2,1)S(1)}, bf16[2048,768]{1,0:T(8,128)(2,1)}, s32[]{:T(128)}, ...), branch_computations={%region_23.24_spmd, %region_24.25_spmd} | conditional | flops 1207959552 | bytes 28901462 | solution.py:279
  503.9 6.6 copy.51
  514.0 7.4 multiply_convert_fusion.1
  546.4 6.5 multiply_reduce_fusion
  553.2 9.5 multiply_convert_fusion
  571.5 5.7 add_convert_fusion
  577.3 7.0 fusion.139
  584.6 8.3 fusion.127
  603.9 43.7 %all-reduce.5.cloned.1.call-done = f32[768,384]{1,0:T(8,128)} async-done(((f32[768,384]{1,0:T(8,128)}), f32[768,384]{1,0:T(8,128)}) %all-reduce.5.cloned.1.call-update) | async-done | bytes 1179664 | tf_op jit(solution)/shard_map/psum | solution.py:302
  649.2 63.5 %reduce-scatter.31.cloned.1.call-done = f32[96,192]{1,0:T(8,128)} async-done(((f32[768,192]{1,0:T(8,128)}), f32[96,192]{1,0:T(8,128)}) %reduce-scatter.31.cloned.1.call-update) | async-done | bytes 73744
  714.3 28.7 %reduce-scatter.21.cloned.1.call-done = bf16[512,384]{1,0:T(8,128)(2,1)} async-done(((bf16[2048,384]{1,0:T(8,128)(2,1)}), bf16[512,384]{1,0:T(8,128)(2,1)}) %reduce-scatter.21.cloned.1.call-update) | async-done | bytes 393232 | tf_op jit(solution)/shard_map/reduce_scatter | solution.py:289
  744.9 38.3 %reduce-scatter.19.cloned.1.call-done = bf16[512,768]{1,0:T(8,128)(2,1)} async-done(((bf16[2048,768]{1,0:T(8,128)(2,1)}), bf16[512,768]{1,0:T(8,128)(2,1)}) %reduce-scatter.19.cloned.1.call-update) | async-done | bytes 786448 | tf_op jit(solution)/shard_map/reduce_scatter | solution.py:283
  785.2 41.1 %all-reduce.2 = (f32[768]{0:T(1024)}, f32[768]{0:T(1024)}, f32[4]{0:T(128)S(1)}) all-reduce(f32[768]{0:T(1024)S(1)} %get-tuple-element.223, f32[768]{0:T(1024)S(1)} %copy-done.86, f32[4]{0:T(128)S(1)} %pad_maximum_fusion.4), channel_id=1, replica_groups=mesh['dp'=8,'tensor'=4] {'dp','tensor'}, use_global_device_ids=true, to_apply=%region_36.37 | all-reduce | flops 1540 | bytes 12320 | tf_op jit(solution)/shard_map/psum | solution.py:302
  831.4 26.2 %reduce-scatter.27.cloned.1.call-done = f32[96,768]{1,0:T(8,128)} async-done(((f32[768,768]{1,0:T(8,128)}), f32[96,768]{1,0:T(8,128)}) %reduce-scatter.27.cloned.1.call-update) | async-done | bytes 294928 | tf_op jit(solution)/shard_map/reduce_scatter | solution.py:299
  857.5 72.6 %reduce-scatter.29.cloned.1.call-done = f32[768,96]{0,1:T(8,128)} async-done(((f32[768,768]{0,1:T(8,128)}), f32[768,96]{0,1:T(8,128)}) %reduce-scatter.29.cloned.1.call-update) | async-done | bytes 294928 | tf_op jit(solution)/shard_map/reduce_scatter | solution.py:300
  930.1 65.9 %reduce-scatter.25.cloned.1.call-done = f32[96,192]{1,0:T(8,128)} async-done(((f32[768,192]{1,0:T(8,128)}), f32[96,192]{1,0:T(8,128)}) %reduce-scatter.25.cloned.1.call-update) | async-done | bytes 73744 | tf_op jit(solution)/shard_map/reduce_scatter | solution.py:297
  996.1 65.4 %reduce-scatter.23.cloned.1.call-done = f32[96,192]{1,0:T(8,128)} async-done(((f32[768,192]{1,0:T(8,128)}), f32[96,192]{1,0:T(8,128)}) %reduce-scatter.23.cloned.1.call-update) | async-done | bytes 73744 | tf_op jit(solution)/shard_map/reduce_scatter | solution.py:296
  (368 shorter events, 164.5 us)
Async XLA Ops:
  8.1 145.5 %all-gather.8.cloned.1.call-start = ((), (), s32[]{:S(2)}) async-start(), calls=%async_computation.10 | async-start | bytes 1966080 | tf_op jit(solution)/shard_map/all_gather | solution.py:184
  10.1 143.4 %all-gather.10.cloned.1.call-start = ((), (), s32[]{:S(2)}) async-start(), calls=%async_computation.11 | async-start | bytes 3932160 | tf_op jit(solution)/shard_map/all_gather | solution.py:183
  15.5 217.0 %reduce-scatter.13.cloned.1.call-start = ((), (), s32[]{:S(2)}) async-start(), calls=%async_computation.12 | async-start | bytes 3932160 | tf_op jit(solution)/shard_map/reduce_scatter | solution.py:200
  194.3 44.5 %all-gather.16.cloned.1.call-start = ((), (), s32[]{:S(2)}) async-start(), calls=%async_computation.15 | async-start | bytes 1327104 | tf_op jit(solution)/shard_map/all_gather | solution.py:177
  194.9 72.3 %all-gather.18.cloned.1.call-start = ((), (), s32[]{:S(2)}) async-start(), calls=%async_computation.17 | async-start | bytes 3932160 | tf_op jit(solution)/shard_map/all_gather | solution.py:231
  195.5 115.6 %all-gather.14.cloned.1.call-start = ((), (), s32[]{:S(2)}) async-start(), calls=%async_computation.14 | async-start | bytes 1327104 | tf_op jit(solution)/shard_map/all_gather | solution.py:176
  196.1 144.1 %all-gather.12.cloned.1.call-start = ((), (), s32[]{:S(2)}) async-start(), calls=%async_computation.13 | async-start | bytes 3932160 | tf_op jit(solution)/shard_map/all_gather | solution.py:206
  234.0 205.0 %copy-start.59 = (f32[512]{0:T(512)}, f32[512]{0:T(512)S(1)}, u32[]{:S(2)}) copy-start(f32[512]{0:T(512)S(1)} %broadcast_multiply_fusion.4) | copy-start | bytes 6148
  235.6 203.4 %copy-start.68 = (f32[512]{0:T(512)}, f32[512]{0:T(512)S(1)}, u32[]{:S(2)}) copy-start(f32[512]{0:T(512)S(1)} %add_rsqrt_fusion) | copy-start | bytes 6148
  236.8 157.2 %reduce-scatter.17.cloned.1.call-start = ((), (), s32[]{:S(2)}) async-start(), calls=%async_computation.18 | async-start | bytes 3932160 | tf_op jit(solution)/shard_map/reduce_scatter | solution.py:236
  356.0 78.5 %reduce-scatter.15.cloned.1.call-start = ((), (), s32[]{:S(2)}) async-start(), calls=%async_computation.16 | async-start | bytes 3932160 | tf_op jit(solution)/shard_map/reduce_scatter | solution.py:210
  365.5 105.1 %all-gather.20.cloned.1.call-start = ((), (), s32[]{:S(2)}) async-start(), calls=%async_computation.19 | async-start | bytes 3932160 | tf_op jit(solution)/shard_map/all_gather | solution.py:241
  442.2 205.4 %all-reduce.5.cloned.1.call-start = ((), (), s32[]{:S(2)}) async-start(), calls=%async_computation.24 | async-start | bytes 2359296 | tf_op jit(solution)/shard_map/psum | solution.py:302
  513.9 198.8 %reduce-scatter.31.cloned.1.call-start = ((), (), s32[]{:S(2)}) async-start(), calls=%async_computation.27 | async-start | bytes 884736
  533.7 209.3 %reduce-scatter.21.cloned.1.call-start = ((), (), s32[]{:S(2)}) async-start(), calls=%async_computation.21 | async-start | bytes 1966080 | tf_op jit(solution)/shard_map/reduce_scatter | solution.py:289
  552.9 230.3 %reduce-scatter.19.cloned.1.call-start = ((), (), s32[]{:S(2)}) async-start(), calls=%async_computation.20 | async-start | bytes 3932160 | tf_op jit(solution)/shard_map/reduce_scatter | solution.py:283
  577.3 280.3 %reduce-scatter.27.cloned.1.call-start = ((), (), s32[]{:S(2)}) async-start(), calls=%async_computation.25 | async-start | bytes 2654208 | tf_op jit(solution)/shard_map/reduce_scatter | solution.py:299
  584.3 345.8 %reduce-scatter.29.cloned.1.call-start = ((), (), s32[]{:S(2)}) async-start(), calls=%async_computation.26 | async-start | bytes 2654208 | tf_op jit(solution)/shard_map/reduce_scatter | solution.py:300
  592.9 403.1 %reduce-scatter.25.cloned.1.call-start = ((), (), s32[]{:S(2)}) async-start(), calls=%async_computation.23 | async-start | bytes 884736 | tf_op jit(solution)/shard_map/reduce_scatter | solution.py:297
  596.8 464.6 %reduce-scatter.23.cloned.1.call-start = ((), (), s32[]{:S(2)}) async-start(), calls=%async_computation.22 | async-start | bytes 884736 | tf_op jit(solution)/shard_map/reduce_scatter | solution.py:296
  600.0 183.3 %copy-start.67 = (f32[512]{0:T(512)S(1)}, f32[512]{0:T(512)}, u32[]{:S(2)}) copy-start(f32[512]{0:T(512)} %copy-done.66) | copy-start | bytes 6148
  600.0 183.3 %copy-start.73 = (f32[768]{0:T(1024)S(1)}, f32[768]{0:T(1024)}, u32[]{:S(2)}) copy-start(f32[768]{0:T(1024)} %param.47) | copy-start | bytes 9220
  600.0 183.3 %copy-start.76 = (f32[512]{0:T(512)S(1)}, f32[512]{0:T(512)}, u32[]{:S(2)}) copy-start(f32[512]{0:T(512)} %copy-done.75) | copy-start | bytes 6148
  603.8 181.4 %copy-start.86 = (f32[768]{0:T(1024)S(1)}, f32[768]{0:T(1024)}, u32[]{:S(2)}) copy-start(f32[768]{0:T(1024)} %get-tuple-element.221) | copy-start | bytes 9220
  603.8 224.3 %copy-start.11 = (bf16[512,768]{1,0:T(8,128)(2,1)S(1)}, bf16[512,768]{1,0:T(8,128)(2,1)}, u32[]{:S(2)}) copy-start(bf16[512,768]{1,0:T(8,128)(2,1)} %reduce-scatter.13.cloned.1.call-done) | copy-start | bytes 2359300
  603.8 224.3 %copy-start.17 = (bf16[512,768]{1,0:T(8,128)(2,1)S(1)}, bf16[512,768]{1,0:T(8,128)(2,1)}, u32[]{:S(2)}) copy-start(bf16[512,768]{1,0:T(8,128)(2,1)} %param.49) | copy-start | bytes 2359300
  603.8 224.3 %copy-start.19 = (bf16[512,768]{1,0:T(8,128)(2,1)S(1)}, bf16[512,768]{1,0:T(8,128)(2,1)}, u32[]{:S(2)}) copy-start(bf16[512,768]{1,0:T(8,128)(2,1)} %reduce-scatter.17.cloned.1.call-done) | copy-start | bytes 2359300
  603.8 224.3 %copy-start.60 = (f32[512]{0:T(512)S(1)}, f32[512]{0:T(512)}, u32[]{:S(2)}) copy-start(f32[512]{0:T(512)} %copy-done.59) | copy-start | bytes 6148
  603.8 224.3 %copy-start.65 = (f32[768]{0:T(1024)S(1)}, f32[768]{0:T(1024)}, u32[]{:S(2)}) copy-start(f32[768]{0:T(1024)} %param.48) | copy-start | bytes 9220
  603.8 224.3 %copy-start.69 = (f32[512]{0:T(512)S(1)}, f32[512]{0:T(512)}, u32[]{:S(2)}) copy-start(f32[512]{0:T(512)} %copy-done.68) | copy-start | bytes 6148
  603.8 224.3 %copy-start.83 = (f32[512]{0:T(512)S(1)}, f32[512]{0:T(512)}, u32[]{:S(2)}) copy-start(f32[512]{0:T(512)} %copy-done.82) | copy-start | bytes 6148
  603.8 224.3 %copy-start.85 = (f32[512]{0:T(512)S(1)}, f32[512]{0:T(512)}, u32[]{:S(2)}) copy-start(f32[512]{0:T(512)} %copy-done.84) | copy-start | bytes 6148
  (98 other events, 1279.5 us)
Sparse Core Ops, SparseCore 0:
  10.5 22.3 all-gather.7
  35.0 28.5 all-gather.9
  194.5 38.0 reduce-scatter.12
  356.1 37.9 reduce-scatter.16
  396.5 37.9 reduce-scatter.14
Sparse Core Ops, SparseCore 1:
  197.2 41.5 all-gather.15
  240.3 26.8 all-gather.17
  269.5 41.5 all-gather.13
  313.3 26.8 all-gather.11
  442.2 28.3 all-gather.19
  514.0 133.5 all-reduce.4
  651.3 61.3 reduce-scatter.30
  715.8 27.1 reduce-scatter.20
  745.4 37.8 reduce-scatter.18
  787.7 69.8 reduce-scatter.26
  861.9 68.2 reduce-scatter.28
  934.4 61.6 reduce-scatter.24
  999.8 61.6 reduce-scatter.22
where the time goes:
time: 1070 us
  waiting for transfers between devices  635 us (59%)
  blocking collectives  172 us (16%)
  matrix products  140 us (13%)
  other arithmetic  63.5 us (6%)
  local copies, waits for them, and re-layouts  37.3 us (3%)
  between operations  18.6 us (2%)
    reduce_scatter x1, waiting for transfers between devices, body(): lax.psum_scatter(grad_down_w, 'dp', scatter_dimension=1, tiled=True)  72.6 us
    reduce_scatter x1, waiting for transfers between devices, body(): lax.psum_scatter(grad_key_w, 'dp', scatter_dimension=0, tiled=True)  65.9 us
    reduce_scatter x1, waiting for transfers between devices, body(): lax.psum_scatter(grad_query_w, 'dp', scatter_dimension=0, tiled=True)  65.4 us
    unnamed x19, waiting for transfers between devices  65.3 us
    psum x1, waiting for transfers between devices, body(): lax.psum((grad_value_w, gain_one_grad, gain_two_grad, squares), ('dp', 't...  43.7 us
    psum x1, blocking collectives, body(): lax.psum((grad_value_w, gain_one_grad, gain_two_grad, squares), ('dp', 't...  41.1 us
    reduce_scatter x1, waiting for transfers between devices, body(): lax.psum_scatter(matmul(hidden, down_w).astype(jnp.bfloat16), 'tensor', s...  40.4 us
    reduce_scatter x1, waiting for transfers between devices, body(): lax.psum_scatter((input_part + value_input).astype(jnp.bfloat16), 'tensor...  38.3 us
  transfers between devices with their start and end apart: 18, of which 16 were waited for; matrix products, arithmetic and copies ran while one was open for 12% of the time, Pallas kernels for 0%

commit v1 on v0

--- a/solution.py
+++ b/solution.py
@@ -3,6 +3,7 @@
 import jax.numpy as jnp
 from jax import lax
 from jax.sharding import PartitionSpec as P
+from jax.lax import axis_index, axis_size, ppermute
 
 HD = 64
 EPS = 1e-05
@@ -203,7 +204,15 @@
     resid_mid = tokens_wide + attn_out
     norm_two, normed_two, inv_two = norm_forward(resid_mid, gain_mlp)
     mlp_input = norm_two.astype(jnp.bfloat16)
-    mlp_rows = lax.all_gather(mlp_input, "tensor", axis=0, tiled=True)
+    wide_n = axis_size("tensor")
+    pages = tuple(((ix, (ix + 1) % wide_n) for ix in range(wide_n)))
+    b_now = [None] * wide_n
+    b_now[wide_n - 1] = mlp_input
+    for b in range(wide_n - 2, -1, -1):
+        b_now[b] = ppermute(b_now[b + 1], "tensor", pages)
+    current_block = jnp.concatenate(b_now, axis=0)
+    z1 = (axis_index("tensor") + 1) * mlp_input.shape[0]
+    mlp_rows = jnp.roll(current_block, z1, axis=0)
     up_pre = matmul(mlp_rows, up_w)
     hidden_act, gelu_pull = jax.vjp(gelu_tanh, up_pre)
     hidden = hidden_act.astype(jnp.bfloat16)

time: 1070 us -> 935 us (0.87)
  waiting for transfers between devices: 635 us -> 485 us
  local copies, waits for them, and re-layouts: 37.3 us -> 50.2 us
    unnamed x19 -> x18, waiting for transfers between devices: 65.3 us -> 1.31 us
    ppermute x0 -> x3, waiting for transfers between devices: none -> 41.2 us  [body(): b_now[b] = ppermute(b_now[b + 1], 'tensor', pages)]
    all_gather x1 -> x0, waiting for transfers between devices: 29.1 us -> none  [body(): mlp_rows = lax.all_gather(mlp_input, 'tensor', axis=0, tiled=True)]
    reduce_scatter x1, waiting for transfers between devices: 28.7 us -> 0.01 us  [body(): lax.psum_scatter(first_part.astype(jnp.bfloat16), 'tensor', scatter_dimen...]
    all_gather x1, waiting for transfers between devices: 28.4 us -> 0.36 us  [body(): cot_rows = lax.all_gather(cotangent, 'tensor', axis=0, tiled=True)]
    reduce_scatter x1, waiting for transfers between devices: 38.3 us -> 15.2 us  [body(): lax.psum_scatter((input_part + value_input).astype(jnp.bfloat16), 'tensor...]
    all_gather x1, waiting for transfers between devices: 36.4 us -> 20.1 us  [body(): lax.all_gather(w_up, 'dp', axis=0, tiled=True)]
    unnamed x225 -> x242, local copies, waits for them, and re-layouts: 22.2 us -> 34.1 us
  transfers between devices with their start and end apart: 18 -> 20, of which waited for: 16 -> 15; matrix products, arithmetic and copies ran while one was open for 12% -> 15% of each run, Pallas kernels for 0% -> 0%
where the time goes in v1:
time: 935 us; the launch traced here: 929 us
  waiting for transfers between devices  485 us (52%)
  blocking collectives  169 us (18%)
  matrix products  140 us (15%)
  other arithmetic  63 us (7%)
  local copies, waits for them, and re-layouts  50.2 us (5%)
  between operations  18.4 us (2%)
    reduce_scatter x1, waiting for transfers between devices, body(): lax.psum_scatter(grad_down_w, 'dp', scatter_dimension=1, tiled=True)  72.2 us
    reduce_scatter x1, waiting for transfers between devices, body(): lax.psum_scatter(grad_query_w, 'dp', scatter_dimension=0, tiled=True)  65.9 us
    reduce_scatter x1, waiting for transfers between devices, body(): lax.psum_scatter(grad_key_w, 'dp', scatter_dimension=0, tiled=True)  65.4 us
    psum x1, waiting for transfers between devices, body(): lax.psum((grad_value_w, gain_one_grad, gain_two_grad, squares), ('dp', 't...  46 us
    ppermute x3, waiting for transfers between devices, body(): b_now[b] = ppermute(b_now[b + 1], 'tensor', pages)  41.2 us
    psum x1, blocking collectives, body(): lax.psum((grad_value_w, gain_one_grad, gain_two_grad, squares), ('dp', 't...  41 us
    reduce_scatter x1, waiting for transfers between devices, body(): lax.psum_scatter(matmul(hidden, down_w).astype(jnp.bfloat16), 'tensor', s...  40.4 us
    reduce_scatter x1, waiting for transfers between devices, body(): lax.psum_scatter(matmul(heads_out, out_w).astype(jnp.bfloat16), 'tensor',...  36.7 us
  transfers between devices with their start and end apart: 20, of which 15 were waited for; matrix products, arithmetic and copies ran while one was open for 15% of the time, Pallas kernels for 0%

profile of v1, /device:TPU:0, one launch (start us, length us, event | category | flops | bytes accessed | tf_op | source)
XLA Modules:
  0.0 929.3 jit_solution(3441304003201086)
XLA Ops:
  16.4 32.9 %all_gather.41 = bf16[192,768]{0,1:T(8,128)(2,1)S(1)} all-gather(bf16[192,96]{0,1:T(8,128)(2,1)S(1)} %copy.36), channel_id=1, replica_groups=mesh['dp'=8,'tensor'=4] {'dp'}, dimensions={1}, use_global_device_ids=true | all-gather | bytes 331776 | tf_op jit(solution)/shard_map/all_gather | solution.py:176
  49.3 31.0 %all_gather.39 = bf16[768,192]{1,0:T(8,128)(2,1)S(1)} all-gather(bf16[96,192]{1,0:T(8,128)(2,1)S(1)} %copy-done.69), channel_id=1, replica_groups=mesh['dp'=8,'tensor'=4] {'dp'}, dimensions={0}, use_global_device_ids=true | all-gather | bytes 331776 | tf_op jit(solution)/shard_map/all_gather | solution.py:173
  80.3 31.1 %all_gather.40 = bf16[768,192]{1,0:T(8,128)(2,1)S(1)} all-gather(bf16[96,192]{1,0:T(8,128)(2,1)S(1)} %copy-done.70), channel_id=1, replica_groups=mesh['dp'=8,'tensor'=4] {'dp'}, dimensions={0}, use_global_device_ids=true | all-gather | bytes 331776 | tf_op jit(solution)/shard_map/all_gather | solution.py:174
  113.9 33.4 %all_gather.37 = bf16[768,384]{1,0:T(8,128)(2,1)} all-gather(bf16[96,384]{1,0:T(8,128)(2,1)S(1)} %copy-done.59), channel_id=1, replica_groups=mesh['dp'=8,'tensor'=4] {'dp'}, dimensions={0}, use_global_device_ids=true | all-gather | bytes 663552 | tf_op jit(solution)/shard_map/all_gather | solution.py:175
  193.4 36.7 %reduce-scatter.13.cloned.1.call-done = bf16[512,768]{1,0:T(8,128)(2,1)} async-done(((bf16[2048,768]{1,0:T(8,128)(2,1)}), bf16[512,768]{1,0:T(8,128)(2,1)}) %reduce-scatter.13.cloned.1.call-update) | async-done | bytes 786448 | tf_op jit(solution)/shard_map/reduce_scatter | solution.py:201
  234.2 11.4 %collective-permute-done = bf16[512,768]{1,0:T(8,128)(2,1)S(1)} collective-permute-done((bf16[512,768]{1,0:T(8,128)(2,1)S(1)}, bf16[512,768]{1,0:T(8,128)(2,1)S(1)}, u32[]{:S(2)}, u32[]{:S(2)}) %collective-permute-start) | collective-permute-done | bytes 786464 | tf_op jit(solution)/shard_map/ppermute | solution.py:212
  245.7 25.8 %collective-permute-done.1 = bf16[512,768]{1,0:T(8,128)(2,1)} collective-permute-done((bf16[512,768]{1,0:T(8,128)(2,1)S(1)}, bf16[512,768]{1,0:T(8,128)(2,1)}, u32[]{:S(2)}, u32[]{:S(2)}) %collective-permute-start.1) | collective-permute-done | bytes 786464 | tf_op jit(solution)/shard_map/ppermute | solution.py:212
  271.9 7.4 fusion.141
  295.4 20.1 %all-gather.11.cloned.1.call-done = bf16[768,768]{1,0:T(8,128)(2,1)} async-done(((bf16[96,768]{1,0:T(8,128)(2,1)}), bf16[768,768]{1,0:T(8,128)(2,1)}) %all-gather.11.cloned.1.call-update) | async-done | bytes 1179664 | tf_op jit(solution)/shard_map/all_gather | solution.py:177
  315.5 11.2 %fusion.17 = (bf16[2048,768]{1,0:T(8,128)(2,1)S(1)}, f32[2048,768]{1,0:T(8,128)}) fusion(f32[2048,768]{1,0:T(8,128)} %fusion.141, bf16[768,768]{1,0:T(8,128)(2,1)} %all-gather.11.cloned.1.call-done, bf16[4096,768]{1,0:T(8,128)(2,1)} %constant_dynamic-update-slice_fusion, s32[]{:T(128)S(6)} %select_n.58), kind=kOutput, calls=%fused_computation.35 | convolution fusion | flops 2447376384 | bytes 20054020 | tf_op jit(solution)/shard_map/dot_general | solution.py:14
  333.7 8.4 convolution_convert_fusion.2
  342.2 26.7 %reduce-scatter.17.cloned.1.call-done = bf16[512,768]{1,0:T(8,128)(2,1)} async-done(((bf16[2048,768]{1,0:T(8,128)(2,1)}), bf16[512,768]{1,0:T(8,128)(2,1)}) %reduce-scatter.17.cloned.1.call-update) | async-done | bytes 786448 | tf_op jit(solution)/shard_map/reduce_scatter | solution.py:245
  368.9 40.4 %reduce-scatter.15.cloned.1.call-done = bf16[512,768]{1,0:T(8,128)(2,1)} async-done(((bf16[2048,768]{1,0:T(8,128)(2,1)}), bf16[512,768]{1,0:T(8,128)(2,1)}) %reduce-scatter.15.cloned.1.call-update) | async-done | bytes 786448 | tf_op jit(solution)/shard_map/reduce_scatter | solution.py:219
  417.4 28.3 %all-gather.17.cloned.1.call-done = bf16[2048,768]{1,0:T(8,128)(2,1)} async-done(((bf16[512,768]{1,0:T(8,128)(2,1)}), bf16[2048,768]{1,0:T(8,128)(2,1)}) %all-gather.17.cloned.1.call-update) | async-done | bytes 3145744 | tf_op jit(solution)/shard_map/all_gather | solution.py:250
  453.0 8.9 multiply_reduce_fusion.1
  468.5 16.6 %conditional.3 = (f32[768,384]{0,1:T(8,128)}, bf16[2048,384]{1,0:T(8,128)(2,1)S(1)}, f32[2048,768]{1,0:T(8,128)}) conditional(s32[]{:T(128)} %convert_element_type.169, (s32[]{:T(128)}, bf16[2048,192]{0,1:T(8,128)(2,1)S(1)}) %tuple.157, (bf16[2048,192]{0,1:T(8,128)(2,1)S(1)}, bf16[2048,768]{1,0:T(8,128)(2,1)}, s32[]{:T(128)}, ...), branch_computations={%region_23.24_spmd, %region_24.25_spmd} | conditional | flops 1207959552 | bytes 28901462 | solution.py:288
  473.7 4.7 convolution_bitcast_fusion
  478.4 6.5 copy.51
  488.6 7.4 multiply_convert_fusion.1
  502.9 5.5 multiply_reduce_fusion.2
  520.6 6.5 multiply_reduce_fusion
  527.5 9.6 %multiply_convert_fusion = bf16[3,512,2048]{2,1,0:T(8,128)(2,1)S(1)} fusion(f32[3,512,2048]{2,1,0:T(8,128)} %get-tuple-element.261, f32[3,512,2048]{2,1,0:T(8,128)} %copy-done, f32[3,512]{1,0:T(4,128)S(1)} %get-tuple-element.260, f32[3,512]{1,0:T(4,128)S(1)} %log_add_fusion), kind=kLoop, calls=%fused_computation.11 | loop fusion | flops 12582912 | bytes 31469568 | tf_op jit(solution)/shard_map/convert_element_type | solution.py:128
  546.0 5.7 add_convert_fusion
  551.8 7.0 fusion.37
  559.0 8.4 fusion.133
  578.6 46.0 %all-reduce.5.cloned.1.call-done = f32[768,384]{1,0:T(8,128)} async-done(((f32[768,384]{1,0:T(8,128)}), f32[768,384]{1,0:T(8,128)}) %all-reduce.5.cloned.1.call-update) | async-done | bytes 1179664 | tf_op jit(solution)/shard_map/psum | solution.py:311
  629.8 15.2 %reduce-scatter.19.cloned.1.call-done = bf16[512,768]{1,0:T(8,128)(2,1)} async-done(((bf16[2048,768]{1,0:T(8,128)(2,1)}), bf16[512,768]{1,0:T(8,128)(2,1)}) %reduce-scatter.19.cloned.1.call-update) | async-done | bytes 786448 | tf_op jit(solution)/shard_map/reduce_scatter | solution.py:292
  647.0 41.0 %all-reduce.2 = (f32[768]{0:T(1024)}, f32[768]{0:T(1024)}, f32[4]{0:T(128)S(1)}) all-reduce(f32[768]{0:T(1024)S(1)} %get-tuple-element.223, f32[768]{0:T(1024)S(1)} %copy-done.91, f32[4]{0:T(128)S(1)} %pad_maximum_fusion.4), channel_id=1, replica_groups=mesh['dp'=8,'tensor'=4] {'dp','tensor'}, use_global_device_ids=true, to_apply=%region_36.37 | all-reduce | flops 1540 | bytes 12320 | tf_op jit(solution)/shard_map/psum | solution.py:311
  693.0 25.5 %reduce-scatter.27.cloned.1.call-done = f32[96,768]{1,0:T(8,128)} async-done(((f32[768,768]{1,0:T(8,128)}), f32[96,768]{1,0:T(8,128)}) %reduce-scatter.27.cloned.1.call-update) | async-done | bytes 294928 | tf_op jit(solution)/shard_map/reduce_scatter | solution.py:308
  718.5 72.2 %reduce-scatter.29.cloned.1.call-done = f32[768,96]{0,1:T(8,128)} async-done(((f32[768,768]{0,1:T(8,128)}), f32[768,96]{0,1:T(8,128)}) %reduce-scatter.29.cloned.1.call-update) | async-done | bytes 294928 | tf_op jit(solution)/shard_map/reduce_scatter | solution.py:309
  790.7 65.4 %reduce-scatter.25.cloned.1.call-done = f32[96,192]{1,0:T(8,128)} async-done(((f32[768,192]{1,0:T(8,128)}), f32[96,192]{1,0:T(8,128)}) %reduce-scatter.25.cloned.1.call-update) | async-done | bytes 73744 | tf_op jit(solution)/shard_map/reduce_scatter | solution.py:306
  856.1 65.9 %reduce-scatter.23.cloned.1.call-done = f32[96,192]{1,0:T(8,128)} async-done(((f32[768,192]{1,0:T(8,128)}), f32[96,192]{1,0:T(8,128)}) %reduce-scatter.23.cloned.1.call-update) | async-done | bytes 73744 | tf_op jit(solution)/shard_map/reduce_scatter | solution.py:305
  (389 shorter events, 168.3 us)
Async XLA Ops:
  8.1 142.8 %all-gather.7.cloned.1.call-start = ((), (), s32[]{:S(2)}) async-start(), calls=%async_computation.10 | async-start | bytes 1966080 | tf_op jit(solution)/shard_map/all_gather | solution.py:185
  8.1 103.2 %copy-start.50 = (s32[2048]{0:T(1024)S(1)}, s32[2048]{0:T(1024)}, u32[]{:S(2)}) copy-start(s32[2048]{0:T(1024)} %param.39) | copy-start | bytes 24580
  10.1 102.3 %slice-start.13 = ((s32[2048]{0:T(1024)}), s32[1024]{0:T(1024)S(1)}, s32[]{:S(2)}) async-start(s32[2048]{0:T(1024)} %param.39), calls=%async_computation.40 | async-start | bytes 8192 | tf_op jit(solution)/shard_map/slice | solution.py:50
  10.1 103.8 %copy-start.59 = (bf16[96,384]{1,0:T(8,128)(2,1)S(1)}, bf16[96,384]{1,0:T(8,128)(2,1)}, u32[]{:S(2)}) copy-start(bf16[96,384]{1,0:T(8,128)(2,1)} %param.43) | copy-start | bytes 221188
  10.1 140.8 %all-gather.9.cloned.1.call-start = ((), (), s32[]{:S(2)}) async-start(), calls=%async_computation.11 | async-start | bytes 3932160 | tf_op jit(solution)/shard_map/all_gather | solution.py:184
  15.5 214.6 %reduce-scatter.13.cloned.1.call-start = ((), (), s32[]{:S(2)}) async-start(), calls=%async_computation.12 | async-start | bytes 3932160 | tf_op jit(solution)/shard_map/reduce_scatter | solution.py:201
  191.8 79.7 %all-gather.13.cloned.1.call-start = ((), (), s32[]{:S(2)}) async-start(), calls=%async_computation.14 | async-start | bytes 1327104 | tf_op jit(solution)/shard_map/all_gather | solution.py:178
  192.4 79.5 %all-gather.15.cloned.1.call-start = ((), (), s32[]{:S(2)}) async-start(), calls=%async_computation.16 | async-start | bytes 3932160 | tf_op jit(solution)/shard_map/all_gather | solution.py:240
  193.0 122.5 %all-gather.11.cloned.1.call-start = ((), (), s32[]{:S(2)}) async-start(), calls=%async_computation.13 | async-start | bytes 1327104 | tf_op jit(solution)/shard_map/all_gather | solution.py:177
  231.6 182.2 %copy-start.55 = (f32[512]{0:T(512)}, f32[512]{0:T(512)S(1)}, u32[]{:S(2)}) copy-start(f32[512]{0:T(512)S(1)} %broadcast_multiply_fusion.4) | copy-start | bytes 6148
  234.1 11.5 %collective-permute-start = (bf16[512,768]{1,0:T(8,128)(2,1)S(1)}, bf16[512,768]{1,0:T(8,128)(2,1)S(1)}, u32[]{:S(2)}, u32[]{:S(2)}) collective-permute-start(bf16[512,768]{1,0:T(8,128)(2,1)S(1)} %multiply_convert_fusion.5), channel_id=1, source_target_pairs={{0,1},{1,2},{2,3},{3,0},{4,5},{5,6},{6,7},{7,4},{8,9},{9,10},{10,1... | collective-permute-start | bytes 2359304 | tf_op jit(solution)/shard_map/ppermute | solution.py:212
  245.6 25.9 %collective-permute-start.1 = (bf16[512,768]{1,0:T(8,128)(2,1)S(1)}, bf16[512,768]{1,0:T(8,128)(2,1)}, u32[]{:S(2)}, u32[]{:S(2)}) collective-permute-start(bf16[512,768]{1,0:T(8,128)(2,1)S(1)} %collective-permute-done), channel_id=1, source_target_pairs={{0,1},{1,2},{2,3},{3,0},{4,5},{5,6},{6,7},{7,4},{8,9},{9,10},{10,1... | collective-permute-start | bytes 2359304 | tf_op jit(solution)/shard_map/ppermute | solution.py:212
  245.6 123.2 %reduce-scatter.17.cloned.1.call-start = ((), (), s32[]{:S(2)}) async-start(), calls=%async_computation.17 | async-start | bytes 3932160 | tf_op jit(solution)/shard_map/reduce_scatter | solution.py:245
  271.5 11.7 %collective-permute-start.2 = (bf16[512,768]{1,0:T(8,128)(2,1)}, bf16[512,768]{1,0:T(8,128)(2,1)}, u32[]{:S(2)}, u32[]{:S(2)}) collective-permute-start(bf16[512,768]{1,0:T(8,128)(2,1)} %collective-permute-done.1), channel_id=1, source_target_pairs={{0,1},{1,2},{2,3},{3,0},{4,5},{5,6},{6,7},{7,4},{8,9},{9,10},{10,1... | collective-permute-start | bytes 2359304 | tf_op jit(solution)/shard_map/ppermute | solution.py:212
  332.5 76.8 %reduce-scatter.15.cloned.1.call-start = ((), (), s32[]{:S(2)}) async-start(), calls=%async_computation.15 | async-start | bytes 3932160 | tf_op jit(solution)/shard_map/reduce_scatter | solution.py:219
  342.1 103.6 %all-gather.17.cloned.1.call-start = ((), (), s32[]{:S(2)}) async-start(), calls=%async_computation.18 | async-start | bytes 3932160 | tf_op jit(solution)/shard_map/all_gather | solution.py:250
  417.0 207.5 %all-reduce.5.cloned.1.call-start = ((), (), s32[]{:S(2)}) async-start(), calls=%async_computation.23 | async-start | bytes 2359296 | tf_op jit(solution)/shard_map/psum | solution.py:311
  488.4 137.8 %reduce-scatter.31.cloned.1.call-start = ((), (), s32[]{:S(2)}) async-start(), calls=%async_computation.26 | async-start | bytes 884736
  508.4 119.4 %reduce-scatter.21.cloned.1.call-start = ((), (), s32[]{:S(2)}) async-start(), calls=%async_computation.20 | async-start | bytes 1966080 | tf_op jit(solution)/shard_map/reduce_scatter | solution.py:298
  527.1 117.9 %reduce-scatter.19.cloned.1.call-start = ((), (), s32[]{:S(2)}) async-start(), calls=%async_computation.19 | async-start | bytes 3932160 | tf_op jit(solution)/shard_map/reduce_scatter | solution.py:292
  551.7 166.8 %reduce-scatter.27.cloned.1.call-start = ((), (), s32[]{:S(2)}) async-start(), calls=%async_computation.24 | async-start | bytes 2654208 | tf_op jit(solution)/shard_map/reduce_scatter | solution.py:308
  558.8 231.9 %reduce-scatter.29.cloned.1.call-start = ((), (), s32[]{:S(2)}) async-start(), calls=%async_computation.25 | async-start | bytes 2654208 | tf_op jit(solution)/shard_map/reduce_scatter | solution.py:309
  567.5 288.7 %reduce-scatter.25.cloned.1.call-start = ((), (), s32[]{:S(2)}) async-start(), calls=%async_computation.22 | async-start | bytes 884736 | tf_op jit(solution)/shard_map/reduce_scatter | solution.py:306
  571.3 350.7 %reduce-scatter.23.cloned.1.call-start = ((), (), s32[]{:S(2)}) async-start(), calls=%async_computation.21 | async-start | bytes 884736 | tf_op jit(solution)/shard_map/reduce_scatter | solution.py:305
  578.5 111.2 %copy-start.11 = (bf16[512,768]{1,0:T(8,128)(2,1)S(1)}, bf16[512,768]{1,0:T(8,128)(2,1)}, u32[]{:S(2)}) copy-start(bf16[512,768]{1,0:T(8,128)(2,1)} %reduce-scatter.13.cloned.1.call-done) | copy-start | bytes 2359300
  578.5 111.2 %copy-start.17 = (bf16[512,768]{1,0:T(8,128)(2,1)S(1)}, bf16[512,768]{1,0:T(8,128)(2,1)}, u32[]{:S(2)}) copy-start(bf16[512,768]{1,0:T(8,128)(2,1)} %param.49) | copy-start | bytes 2359300
  578.5 111.2 %copy-start.19 = (bf16[512,768]{1,0:T(8,128)(2,1)S(1)}, bf16[512,768]{1,0:T(8,128)(2,1)}, u32[]{:S(2)}) copy-start(bf16[512,768]{1,0:T(8,128)(2,1)} %reduce-scatter.17.cloned.1.call-done) | copy-start | bytes 2359300
  578.5 111.2 %copy-start.56 = (f32[512]{0:T(512)S(1)}, f32[512]{0:T(512)}, u32[]{:S(2)}) copy-start(f32[512]{0:T(512)} %copy-done.55) | copy-start | bytes 6148
  578.5 111.2 %copy-start.63 = (f32[768]{0:T(1024)S(1)}, f32[768]{0:T(1024)}, u32[]{:S(2)}) copy-start(f32[768]{0:T(1024)} %param.48) | copy-start | bytes 9220
  578.5 111.2 %copy-start.68 = (f32[512]{0:T(512)S(1)}, f32[512]{0:T(512)}, u32[]{:S(2)}) copy-start(f32[512]{0:T(512)} %copy-done.66) | copy-start | bytes 6148
  578.6 111.2 %copy-start.88 = (f32[512]{0:T(512)S(1)}, f32[512]{0:T(512)}, u32[]{:S(2)}) copy-start(f32[512]{0:T(512)} %copy-done.87) | copy-start | bytes 6148
  578.6 111.2 %copy-start.90 = (f32[512]{0:T(512)S(1)}, f32[512]{0:T(512)}, u32[]{:S(2)}) copy-start(f32[512]{0:T(512)} %copy-done.89) | copy-start | bytes 6148
  (105 other events, 1281.6 us)
Sparse Core Ops, SparseCore 0:
  10.4 22.3 all-gather.6
  35.0 28.5 all-gather.8
  191.9 38.1 reduce-scatter.12
  417.1 28.5 all-gather.16
  488.5 136.0 all-reduce.4
Sparse Core Ops, SparseCore 1:
  194.5 41.7 all-gather.12
  237.6 34.2 all-gather.14
  274.0 41.5 all-gather.10
  332.6 36.2 reduce-scatter.16
  371.4 37.8 reduce-scatter.14
  508.5 65.6 reduce-scatter.30
  577.1 27.4 reduce-scatter.20
  607.1 37.8 reduce-scatter.18
  648.9 69.5 reduce-scatter.26
  722.6 68.0 reduce-scatter.28
  794.4 61.6 reduce-scatter.24
  860.4 61.6 reduce-scatter.22
